TPU v7x, 256 devices: a whole 4x4x8 slice. The times are simulated.
256 devices in a mesh: blk: 32 (over x, z), leaf: 4 (over y), samp: 2 (over core).
Axes of the slice: x: 4, y: 4, z: 8, core: 2. Of those that a mesh axis runs over, the one named last changes fastest.
Arguments:
- points: float32 [3, 32768], P(None, ('blk', 'leaf')), may hold values from 0 to 64, as said below
- neighbors: int32 [128, 8], P(('blk', 'leaf')), may hold values from -1 to 127, as said below
- omega: float32 [512, 32768], P(None, ('blk', 'leaf')), may hold values from -6 to 6
- observed: float32 [32768], P(('blk', 'leaf')), may hold values from -6 to 6
- prior_draws: float32 [64, 32768], P('samp', ('blk', 'leaf')), may hold values from -6 to 6
Outputs:
- weights: float32 [64, 32768], P('samp', ('blk', 'leaf'))
- residual: float32 [64, 32768], P('samp', ('blk', 'leaf'))
Inputs may be any that keep to these rules, and one draw needn't show every extreme that they name: Block g's points lie in the unit cell with integer corner (cx, cy, cz), where cx // 2 = g // 4 and 0 <= cy, cz < 3. `neighbors`: row g lists in ascending order every block h whose unit cell touches g's (cells at most one apart in every coordinate, the first taken periodic of period 2 * 32), which includes every block with a point within distance 1 of a point of g, followed by -1 in the unused slots; the relation is symmetric, and every listed block has a slab index h // 4 equal to or cyclically next to g // 4.
All inputs are finite; a program needn't handle non-finite values.
Results may differ from a plain program's by a relative error of at most 0.0003.
Values sent between devices are 32-bit elements; how exact they have to be, the bound alone decides.
A program may use at most 64 MiB of HBM per device.

v0:
```python
import jax
import jax.numpy as jnp
from jax import lax
from jax.sharding import PartitionSpec as P

PB = 256
ITERS = 2
support_radius = 0.8
noise_variance = 1.0
sketch_shift = 1.0
ALL_AXES = ("blk", "leaf", "samp")


def shifted_2(block, axis, distance):
    devices = range(lax.axis_size(axis))
    route = [((i - distance) % len(devices), i) for i in devices]
    return lax.ppermute(block, axis, route)


def wendland(row_points, column_points, period):
    offset = row_points[None, :, :, None] - column_points[:, :, None, :]
    half_period = 0.5 * period
    along_x = jnp.mod(offset[:, 0] + half_period, period) - half_period
    squared = along_x * along_x + offset[:, 1] * offset[:, 1] + offset[:, 2] * offset[:, 2]
    radius = jnp.sqrt(squared) / support_radius
    remain = jnp.maximum(1.0 - radius, 0.0)
    return remain**4 * (4.0 * radius + 1.0)


def high_dot(left, right):
    return jnp.dot(left, right, precision=lax.Precision.HIGHEST, preferred_element_type=jnp.float32)


def shifted(values, offset_by):
    return shifted_2(values, "blk", offset_by)


def beside_all(values):
    slab_values = lax.all_gather(values, "leaf", axis=1, tiled=True)
    return jnp.concatenate([shifted(slab_values, 1), slab_values, shifted(slab_values, -1)], axis=1)


def lower_solve(factor, values):
    return lax.linalg.triangular_solve(factor, values, left_side=True, lower=True)


def local(points, neighbors, omega, observed, prior_draws):
    blk_dev = neighbors.shape[0]
    cycle_count = lax.axis_size("blk")
    slab_blocks = blk_dev * lax.axis_size("leaf")
    period = 2.0 * cycle_count
    own_slab = lax.axis_index("blk")
    n_samp = lax.axis_size("samp")
    samp_idx = lax.axis_index("samp")
    usable = neighbors >= 0
    relative = jnp.mod(neighbors // slab_blocks - own_slab + 1, cycle_count)
    chosen = jnp.where(usable, relative * slab_blocks + jnp.mod(neighbors, slab_blocks), 0)
    usable_weight = usable.astype(jnp.float32)
    reach_points = beside_all(points)
    reach_blocks = reach_points.reshape(3, 3 * slab_blocks, PB).transpose(1, 0, 2)
    row_blocks = points.reshape(3, blk_dev, PB).transpose(1, 0, 2)
    kernel_tile = wendland(row_blocks[0], reach_blocks[chosen[0]], period)
    kernel_tile = kernel_tile * usable_weight[0][:, None, None]

    def apply_kernel(values):
        width = values.shape[0]
        reach = beside_all(values).reshape(width, 3 * slab_blocks, PB)
        picked = jnp.take(reach, chosen[0], axis=1)
        return jnp.einsum("cnj,nij->ci", picked, kernel_tile, precision=lax.Precision.HIGHEST)

    def slot(x):
        zeros = jnp.zeros((n_samp,) + x.shape, x.dtype)
        return lax.dynamic_update_index_in_dim(zeros, x, samp_idx, 0)

    def unslot(xs):
        return lax.dynamic_index_in_dim(xs, samp_idx, 0, keepdims=False)

    def total_per_samp(values):
        return jax.tree.map(unslot, lax.psum(jax.tree.map(slot, values), ALL_AXES))

    sketch = apply_kernel(omega) + sketch_shift * omega
    rhs = observed[None, :] - prior_draws
    half = PB // n_samp
    omega_half = lax.dynamic_slice_in_dim(omega, samp_idx * half, half, axis=1)
    sketch_half = lax.dynamic_slice_in_dim(sketch, samp_idx * half, half, axis=1)
    core_part = high_dot(omega_half, sketch_half.T)
    square_part = high_dot(sketch_half, sketch_half.T)
    joint_part = 0.5 * (core_part + core_part.T) + 0.5 * (square_part + square_part.T)
    rhs_part = slot(high_dot(sketch, rhs.T))
    joint_gram, rhs_proj = lax.psum((joint_part, rhs_part), ALL_AXES)
    rhs_proj = unslot(rhs_proj)
    joint_factor = jnp.linalg.cholesky(joint_gram)

    def precond_from(vectors, projected):
        first_solve = lower_solve(joint_factor, projected)
        solved = lax.linalg.triangular_solve(
            joint_factor, first_solve, left_side=True, lower=True, transpose_a=True
        )
        return (vectors - high_dot(solved.T, sketch)) / noise_variance

    residual = rhs
    projected = rhs_proj
    precond = precond_from(residual, projected)
    direction = precond
    weights = jnp.zeros_like(rhs)
    image = apply_kernel(direction) + noise_variance * direction
    inner_now, curvature, image_proj = total_per_samp(
        (
            jnp.sum(residual * precond, axis=1),
            jnp.sum(direction * image, axis=1),
            high_dot(sketch, image.T),
        )
    )
    step_size = inner_now / curvature
    weights = weights + step_size[:, None] * direction
    residual = residual - step_size[:, None] * image
    projected = projected - step_size[None, :] * image_proj
    precond = precond_from(residual, projected)
    inner_next = total_per_samp(jnp.sum(residual * precond, axis=1))
    direction = precond + (inner_next / inner_now)[:, None] * direction
    inner_now = inner_next
    image = apply_kernel(direction) + noise_variance * direction
    curvature = total_per_samp(jnp.sum(direction * image, axis=1))
    step_size = inner_now / curvature
    weights = weights + step_size[:, None] * direction
    residual = residual - step_size[:, None] * image
    return (weights, residual)


def solution(mesh):
    in_specs = (
        P(None, ("blk", "leaf")),
        P(("blk", "leaf"), None),
        P(None, ("blk", "leaf")),
        P(("blk", "leaf")),
        P("samp", ("blk", "leaf")),
    )
    out_specs = (P("samp", ("blk", "leaf")), P("samp", ("blk", "leaf")))
    return jax.shard_map(local, mesh=mesh, in_specs=in_specs, out_specs=out_specs, check_vma=False)
```

profile of v0, /device:TPU:1, one launch (start us, length us, event | category | flops | bytes accessed | tf_op | source)
XLA Modules:
  0.0 1005.4 jit_solution(9335899095662480256)
XLA Ops:
  7.2 2.0 copy.10
  9.3 10.5 %all_gather.13 = f32[3,1024]{1,0:T(4,128)S(1)} all-gather(f32[3,256]{1,0:T(4,128)} %param.11), channel_id=1, replica_groups=mesh['blk'=32,'leaf'=4,'samp'=2] {'leaf'}, dimensions={1}, use_global_device_ids=true | all-gather | bytes 15360 | tf_op jit(solution)/shard_map/all_gather | solution.py:39
  19.9 7.8 collective-permute-start.3
  27.6 19.4 %all-gather.2.cloned.1.call-done = f32[512,1024]{0,1:T(8,128)} async-done(((f32[512,256]{0,1:T(8,128)}), f32[512,1024]{0,1:T(8,128)}) %all-gather.2.cloned.1.call-update) | async-done | bytes 2097168 | tf_op jit(solution)/shard_map/all_gather | solution.py:39
  47.1 5.2 collective-permute-start.1
  54.4 1.3 broadcast_subtract_fusion
  55.7 2.6 multiply_multiply_fusion
  58.3 38.5 %collective-permute-done.1 = f32[512,1024]{0,1:T(8,128)} collective-permute-done((f32[512,1024]{0,1:T(8,128)}, f32[512,1024]{0,1:T(8,128)}, u32[]{:S(2)}, u32[]{:S(2)}) %collective-permute-start.1) | collective-permute-done | bytes 2097184 | tf_op jit(solution)/shard_map/ppermute | solution.py:17
  96.8 5.4 collective-permute-done
  102.2 5.6 pad_maximum_fusion
  107.8 6.5 copy.11
  114.3 5.6 gather_fusion
  119.9 5.5 fusion.17
  125.4 2.0 fusion.34
  127.3 2.0 fusion.32
  129.4 2.5 copy.13
  131.9 2.5 copy.14
  134.5 3.7 fusion.26
  139.7 250.3 %all-reduce.8.cloned.1.call-done = (f32[512,512]{1,0:T(8,128)}, f32[2,512,32]{1,2,0:T(8,128)}) async-done(((f32[512,512]{1,0:T(8,128)}, f32[2,512,32]{1,2,0:T(8,128)}), (f32[512,512]{1,0:T(8,128)}, f32[2,512,32]{1,2,0:T(8,128)})) %all-reduce.8.cloned.1.call-update) | async-done | bytes 1179664 | tf_op jit(solution)/shard_map/psum | solution.py:90
  390.8 2.6 copy.15
  393.4 1.8 fusion.24
  396.2 11.7 %cholesky.104 = f32[128,128]{1,0:T(8,128)S(1)} custom-call(f32[128,128]{1,0:T(8,128)S(1)} %cholesky.266), custom_call_target="Cholesky" | custom-call | tf_op jit(solution)/shard_map/jit(cholesky)/cholesky | solution.py:92
  407.9 9.8 custom-call.33
  417.7 1.2 cholesky.224
  418.9 2.0 constant_dynamic-update-slice_fusion
  420.9 1.2 convolution_subtract_fusion
  422.1 11.7 %cholesky.217 = f32[128,128]{1,0:T(8,128)S(1)} custom-call(f32[128,128]{1,0:T(8,128)S(1)} %cholesky.270), custom_call_target="Cholesky" | custom-call | tf_op jit(solution)/shard_map/jit(cholesky)/cholesky | solution.py:92
  434.5 10.2 %custom-call.34 = f32[1,128,128]{1,2,0:T(8,128)S(1)} custom-call(f32[1,128,128]{2,1,0:T(8,128)S(1)} %get-tuple-element.61), custom_call_target="InvertDiagBlocksLowerTriangular" | custom-call | tf_op jit(solution)/shard_map/jit(cholesky)/cholesky | solution.py:92
  445.7 1.4 convolution_subtract_fusion.1
  447.1 11.7 %cholesky.238 = f32[128,128]{1,0:T(8,128)S(1)} custom-call(f32[128,128]{1,0:T(8,128)S(1)} %cholesky.275), custom_call_target="Cholesky" | custom-call | tf_op jit(solution)/shard_map/jit(cholesky)/cholesky | solution.py:92
  460.2 9.8 custom-call.35
  470.9 1.4 convolution_subtract_fusion.2
  472.3 11.7 %cholesky.255 = f32[128,128]{1,0:T(8,128)S(1)} custom-call(f32[128,128]{1,0:T(8,128)S(1)} %convolution_subtract_fusion.2), custom_call_target="Cholesky" | custom-call | tf_op jit(solution)/shard_map/jit(cholesky)/cholesky | solution.py:92
  488.6 2.5 select_select_fusion
  491.1 12.0 %while.8 = (s32[]{:T(128)}, f32[512,512]{1,0:T(8,128)}, s32[4,2]{0,1:T(2,128)S(1)}, f32[4,128,128]{2,1,0:T(8,128)S(1)}, s32[]{:T(128)}) while((s32[]{:T(128)}, f32[512,512]{1,0:T(8,128)}, s32[4,2]{0,1:T(2,128)S(1)}, f32[4,128,128]{2,1,0:T(8,128)S(1)}, s32[]{:T(128)}) %tuple.51), condition=%wide.while_cond.1, body=%wide.while_body.1.sunk | while | flops 2 | bytes 131189 | solution.py:96
  491.7 2.3 bitcast_dynamic-update-slice_fusion.2
  494.8 2.3 bitcast_dynamic-update-slice_fusion.2
  497.8 2.3 bitcast_dynamic-update-slice_fusion.2
  500.8 2.3 bitcast_dynamic-update-slice_fusion.2
  503.1 39.3 %custom-call.39 = f32[4,128,128]{1,2,0:T(8,128)S(1)} custom-call(f32[4,128,128]{2,1,0:T(8,128)S(1)} %get-tuple-element.34), custom_call_target="InvertDiagBlocksLowerTriangular" | custom-call | tf_op jit(solution)/shard_map/triangular_solve/custom-call.8 | solution.py:96
  542.6 1.0 convolution_subtract_fusion.16
  543.8 1.1 convolution_subtract_fusion.15
  545.2 1.3 convolution_subtract_fusion.14
  548.0 1.1 convolution_subtract_fusion.12
  549.4 1.2 convolution_subtract_fusion.11
  551.2 9.2 all_gather.14
  560.4 5.0 collective-permute-start.5
  565.4 1.9 collective-permute-done.5
  567.4 5.2 collective-permute-done.4
  573.2 2.8 multiply_reduce_fusion.3
  577.5 76.1 %all-reduce.1 = (f32[2,32]{1,0:T(2,128)S(1)}, f32[2,32]{1,0:T(2,128)S(1)}) all-reduce(f32[2,32]{1,0:T(2,128)S(1)} %dynamic_update_slice.22, f32[2,32]{1,0:T(2,128)S(1)} %dynamic_update_slice.21), channel_id=1, replica_groups=mesh['blk'=32,'leaf'=4,'samp'=2] {'blk','leaf','samp'}, use_global_device_ids=true, to_apply=%region_13.17 | all-reduce | flops 128 | bytes 1024 | tf_op jit(solution)/shard_map/psum | solution.py:79
  653.7 161.9 %all-reduce.6.cloned.1.call-done = f32[2,512,32]{1,2,0:T(8,128)} async-done(((f32[2,512,32]{1,2,0:T(8,128)}), f32[2,512,32]{1,2,0:T(8,128)}) %all-reduce.6.cloned.1.call-update) | async-done | bytes 131088 | tf_op jit(solution)/shard_map/psum | solution.py:79
  816.7 1.0 convolution_subtract_fusion.10
  817.9 1.2 convolution_subtract_fusion.9
  819.2 1.3 convolution_subtract_fusion.8
  822.1 1.1 convolution_subtract_fusion.6
  823.4 1.2 convolution_subtract_fusion.5
  825.4 75.9 %psum.54 = f32[2,32]{1,0:T(2,128)S(1)} all-reduce(f32[2,32]{1,0:T(2,128)S(1)} %dynamic_update_slice.24), channel_id=1, replica_groups=mesh['blk'=32,'leaf'=4,'samp'=2] {'blk','leaf','samp'}, use_global_device_ids=true, to_apply=%region_16.20 | all-reduce | flops 64 | bytes 512 | tf_op jit(solution)/shard_map/psum | solution.py:79
  901.4 9.1 all_gather.15
  910.5 1.4 collective-permute-start.7
  912.1 2.4 collective-permute-done.7
  914.5 4.6 collective-permute-done.6
  919.7 2.0 multiply_reduce_fusion
  921.8 76.2 %psum.55 = f32[2,32]{1,0:T(2,128)S(1)} all-reduce(f32[2,32]{1,0:T(2,128)S(1)} %dynamic_update_slice.25), channel_id=1, replica_groups=mesh['blk'=32,'leaf'=4,'samp'=2] {'blk','leaf','samp'}, use_global_device_ids=true, to_apply=%region_18.22 | all-reduce | flops 64 | bytes 512 | tf_op jit(solution)/shard_map/psum | solution.py:79
  (112 shorter events, 24.6 us)
Async XLA Ops:
  7.2 39.9 %all-gather.2.cloned.1.call-start = ((), (), s32[]{:S(2)}) async-start(), calls=%async_computation | async-start | bytes 2621440 | tf_op jit(solution)/shard_map/all_gather | solution.py:39
  9.3 380.7 %all-reduce.8.cloned.1.call-start = ((), (), s32[]{:S(2)}) async-start(), calls=%async_computation.2 | async-start | bytes 2359296 | tf_op jit(solution)/shard_map/psum | solution.py:90
  19.9 33.9 %collective-permute-start.3 = (f32[3,1024]{1,0:T(4,128)S(1)}, f32[3,1024]{1,0:T(4,128)S(1)}, u32[]{:S(2)}, u32[]{:S(2)}) collective-permute-start(f32[3,1024]{1,0:T(4,128)S(1)} %all_gather.13), channel_id=1, source_target_pairs={{8,0},{16,8},{24,16},{32,24},{40,32},{48,40},{56,48},{64,56},{72,6... | collective-permute-start | bytes 36872 | tf_op jit(solution)/shard_map/ppermute | solution.py:17
  27.6 26.1 %collective-permute-start.2 = (f32[3,1024]{1,0:T(4,128)S(1)}, f32[3,1024]{1,0:T(4,128)S(1)}, u32[]{:S(2)}, u32[]{:S(2)}) collective-permute-start(f32[3,1024]{1,0:T(4,128)S(1)} %all_gather.13), channel_id=1, source_target_pairs={{248,0},{0,8},{8,16},{16,24},{24,32},{32,40},{40,48},{48,56},{56,6... | collective-permute-start | bytes 36872 | tf_op jit(solution)/shard_map/ppermute | solution.py:17
  47.1 49.8 %collective-permute-start.1 = (f32[512,1024]{0,1:T(8,128)}, f32[512,1024]{0,1:T(8,128)}, u32[]{:S(2)}, u32[]{:S(2)}) collective-permute-start(f32[512,1024]{0,1:T(8,128)} %all-gather.2.cloned.1.call-done), channel_id=1, source_target_pairs={{8,0},{16,8},{24,16},{32,24},{40,32},{48,40},{56,48},{64,56},{72,6... | collective-permute-start | bytes 6291464 | tf_op jit(solution)/shard_map/ppermute | solution.py:17
  52.2 50.0 %collective-permute-start = (f32[512,1024]{0,1:T(8,128)}, f32[512,1024]{0,1:T(8,128)}, u32[]{:S(2)}, u32[]{:S(2)}) collective-permute-start(f32[512,1024]{0,1:T(8,128)} %all-gather.2.cloned.1.call-done), channel_id=1, source_target_pairs={{248,0},{0,8},{8,16},{16,24},{24,32},{32,40},{40,48},{48,56},{56,6... | collective-permute-start | bytes 6291464 | tf_op jit(solution)/shard_map/ppermute | solution.py:17
  55.7 46.5 %copy-start.2 = (f32[512,1024]{0,1:T(8,128)S(1)}, f32[512,1024]{0,1:T(8,128)}, u32[]{:S(2)}) copy-start(f32[512,1024]{0,1:T(8,128)} %all-gather.2.cloned.1.call-done) | copy-start | bytes 6291460
  114.3 5.6 copy-start
  134.5 3.7 copy-start.5
  134.5 3.7 copy-start.10
  138.8 0.6 copy-start.7
  139.4 676.2 %all-reduce.6.cloned.1.call-start = ((), (), s32[]{:S(2)}) async-start(), calls=%async_computation.1 | async-start | bytes 262144 | tf_op jit(solution)/shard_map/psum | solution.py:79
  395.2 1.0 copy-start.1
  551.2 16.2 %copy-start.3 = (f32[32,256]{1,0:T(8,128)}, f32[32,256]{1,0:T(8,128)S(1)}, u32[]{:S(2)}) copy-start(f32[32,256]{1,0:T(8,128)S(1)} %convolution_subtract_fusion.4) | copy-start | bytes 98308
  560.4 7.0 collective-permute-start.5
  565.4 7.1 collective-permute-start.4
  573.2 80.4 %copy-start.6 = (f32[32,256]{1,0:T(8,128)S(1)}, f32[32,256]{1,0:T(8,128)}, u32[]{:S(2)}) copy-start(f32[32,256]{1,0:T(8,128)} %param.15) | copy-start | bytes 98308
  573.2 242.4 %copy-start.9 = (f32[2,512,32]{1,2,0:T(8,128)S(1)}, f32[2,512,32]{1,2,0:T(8,128)}, u32[]{:S(2)}) copy-start(f32[2,512,32]{1,2,0:T(8,128)} %get-tuple-element.50) | copy-start | bytes 393220
  576.1 325.3 %copy-start.4 = (f32[32,256]{1,0:T(8,128)S(1)}, f32[32,256]{1,0:T(8,128)}, u32[]{:S(2)}) copy-start(f32[32,256]{1,0:T(8,128)} %copy-done.3) | copy-start | bytes 98308
  576.7 0.7 copy-start.8
  910.5 4.0 collective-permute-start.7
  911.9 7.1 collective-permute-start.6
Sparse Core Ops, SparseCore 0:
  9.8 37.2 all-gather.1
  139.5 250.3 all-reduce.7
  577.5 238.0 all-reduce.5
where the time goes:
time: 1010 us
  waiting for transfers between devices  490 us (49%)
  blocking collectives  257 us (25%)
  other arithmetic  141 us (14%)
  matrix products  40.6 us (4%)
  local copies, waits for them, and re-layouts  40.1 us (4%)
  starting transfers between devices  20.1 us (2%)
  between operations  17.2 us (2%)
    psum x1, waiting for transfers between devices, local(): joint_gram, rhs_proj = lax.psum((joint_part, rhs_part), ALL_AXES)  250 us
    psum x3, blocking collectives, total_per_samp(): return jax.tree.map(unslot, lax.psum(jax.tree.map(slot, values), ALL_AXES))  228 us
    psum x1, waiting for transfers between devices, total_per_samp(): return jax.tree.map(unslot, lax.psum(jax.tree.map(slot, values), ALL_AXES))  162 us
    another operation x14, other arithmetic, local(): joint_factor = jnp.linalg.cholesky(joint_gram)  80.7 us
    ppermute x8, waiting for transfers between devices, shifted_2(): return lax.ppermute(block, axis, route)  57.9 us
    another operation x4, other arithmetic, precond_from(): lax.linalg.triangular_solve(joint_factor, first_solve, left_side=True, lo...  41.8 us
    all_gather x3, blocking collectives, beside_all(): slab_values = lax.all_gather(values, 'leaf', axis=1, tiled=True)  28.8 us
  transfers between devices with their start and end apart: 11, of which 9 were waited for; matrix products, arithmetic and copies ran while one was open for 1% of the time, Pallas kernels for 0%

commit v1 on v0

--- a/solution.py
+++ b/solution.py
@@ -9,6 +9,16 @@
 noise_variance = 1.0
 sketch_shift = 1.0
 ALL_AXES = ("blk", "leaf", "samp")
+
+
+def pass_along(block, axis, along):
+    count = lax.axis_size(axis)
+    current, parts = (block, [block])
+    for _ in range(count - 1):
+        current = lax.ppermute(current, axis, [(i, (i + 1) % count) for i in range(count)])
+        parts.insert(0, current)
+    row_of_blocks = jnp.concatenate(parts, axis=along)
+    return jnp.roll(row_of_blocks, (lax.axis_index(axis) + 1) * block.shape[along], axis=along)
 
 
 def shifted_2(block, axis, distance):
@@ -36,7 +46,7 @@
 
 
 def beside_all(values):
-    slab_values = lax.all_gather(values, "leaf", axis=1, tiled=True)
+    slab_values = pass_along(values, "leaf", 1)
     return jnp.concatenate([shifted(slab_values, 1), slab_values, shifted(slab_values, -1)], axis=1)
 
 

time: 1010 us -> 1030 us (1.020)
  waiting for transfers between devices: 490 us -> 512 us
  blocking collectives: 257 us -> 240 us
  starting transfers between devices: 20.1 us -> 34.4 us
    ppermute x0 -> x12, waiting for transfers between devices: none -> 52.6 us  [pass_along(): lax.ppermute(current, axis, [(i, (i + 1) % count) for i in range(count)])]
    all_gather x3 -> x0, blocking collectives: 28.8 us -> none  [beside_all(): slab_values = lax.all_gather(values, 'leaf', axis=1, tiled=True)]
    all_gather x1 -> x0, waiting for transfers between devices: 19.4 us -> none  [beside_all(): slab_values = lax.all_gather(values, 'leaf', axis=1, tiled=True)]
    ppermute x8, waiting for transfers between devices: 57.9 us -> 42.9 us  [shifted_2(): return lax.ppermute(block, axis, route)]
    psum x3, blocking collectives: 228 us -> 240 us  [total_per_samp(): return jax.tree.map(unslot, lax.psum(jax.tree.map(slot, values), ALL_AXES))]
  transfers between devices with their start and end apart: 11 -> 22, of which waited for: 9 -> 15; matrix products, arithmetic and copies ran while one was open for 1% -> 1% of each run, Pallas kernels for 0% -> 0%
where the time goes in v1:
time: 1030 us; the launch traced here: 1020 us
  waiting for transfers between devices  512 us (50%)
  blocking collectives  240 us (23%)
  other arithmetic  140 us (14%)
  matrix products  40.6 us (4%)
  local copies, waits for them, and re-layouts  39.6 us (4%)
  starting transfers between devices  34.4 us (3%)
  between operations  17.8 us (2%)
    psum x1, waiting for transfers between devices, local(): joint_gram, rhs_proj = lax.psum((joint_part, rhs_part), ALL_AXES)  256 us
    psum x3, blocking collectives, total_per_samp(): return jax.tree.map(unslot, lax.psum(jax.tree.map(slot, values), ALL_AXES))  240 us
    psum x1, waiting for transfers between devices, total_per_samp(): return jax.tree.map(unslot, lax.psum(jax.tree.map(slot, values), ALL_AXES))  161 us
    another operation x14, other arithmetic, local(): joint_factor = jnp.linalg.cholesky(joint_gram)  80.4 us
    ppermute x12, waiting for transfers between devices, pass_along(): lax.ppermute(current, axis, [(i, (i + 1) % count) for i in range(count)])  52.6 us
    ppermute x8, waiting for transfers between devices, shifted_2(): return lax.ppermute(block, axis, route)  42.9 us
    another operation x4, other arithmetic, precond_from(): lax.linalg.triangular_solve(joint_factor, first_solve, left_side=True, lo...  41.8 us
    ppermute x8, starting transfers between devices, shifted_2(): return lax.ppermute(block, axis, route)  24.8 us
  transfers between devices with their start and end apart: 22, of which 15 were waited for; matrix products, arithmetic and copies ran while one was open for 1% of the time, Pallas kernels for 0%

profile of v1, /device:TPU:1, one launch (start us, length us, event | category | flops | bytes accessed | tf_op | source)
XLA Modules:
  0.0 1024.6 jit_solution(8591914442298133993)
XLA Ops:
  7.2 1.2 copy.10
  8.5 2.2 collective-permute-start
  10.7 11.0 %collective-permute-done = f32[512,256]{0,1:T(8,128)S(1)} collective-permute-done((f32[512,256]{0,1:T(8,128)S(1)}, f32[512,256]{0,1:T(8,128)S(1)}, u32[]{:S(2)}, u32[]{:S(2)}) %collective-permute-start) | collective-permute-done | bytes 524320 | tf_op jit(solution)/shard_map/ppermute | solution.py:18
  21.7 1.6 collective-permute-start.1
  23.3 1.5 collective-permute-start.5
  26.1 8.1 collective-permute-done.5
  35.0 1.7 collective-permute-start.2
  37.9 9.0 collective-permute-done.7
  47.3 1.5 constant_dynamic-slice_fusion.6
  48.8 3.9 collective-permute-start.3
  52.7 6.1 collective-permute-start.4
  59.0 5.0 collective-permute-start.9
  64.0 38.1 %collective-permute-done.8 = f32[3,1024]{1,0:T(4,128)S(1)} collective-permute-done((f32[3,1024]{1,0:T(4,128)S(1)}, f32[3,1024]{1,0:T(4,128)S(1)}, u32[]{:S(2)}, u32[]{:S(2)}) %collective-permute-start.8) | collective-permute-done | bytes 12320 | tf_op jit(solution)/shard_map/ppermute | solution.py:27
  103.3 2.6 multiply_multiply_fusion
  106.0 6.2 pad_maximum_fusion
  112.2 6.5 copy.13
  118.7 5.6 gather_fusion
  124.3 5.5 fusion.17
  129.8 2.0 fusion.32
  131.8 2.0 fusion.34
  133.7 2.6 copy.15
  136.3 2.6 copy.16
  138.9 3.7 fusion.26
  144.3 256.0 %all-reduce.8.cloned.1.call-done = (f32[512,512]{1,0:T(8,128)}, f32[2,512,32]{1,2,0:T(8,128)}) async-done(((f32[512,512]{1,0:T(8,128)}, f32[2,512,32]{1,2,0:T(8,128)}), (f32[512,512]{1,0:T(8,128)}, f32[2,512,32]{1,2,0:T(8,128)})) %all-reduce.8.cloned.1.call-update) | async-done | bytes 1179664 | tf_op jit(solution)/shard_map/psum | solution.py:100
  400.3 2.6 copy.17
  402.9 1.8 fusion.24
  405.6 11.7 %cholesky.104 = f32[128,128]{1,0:T(8,128)S(1)} custom-call(f32[128,128]{1,0:T(8,128)S(1)} %cholesky.266), custom_call_target="Cholesky" | custom-call | tf_op jit(solution)/shard_map/jit(cholesky)/cholesky | solution.py:102
  418.5 9.8 custom-call.33
  428.3 1.9 constant_dynamic-update-slice_fusion.16
  430.3 1.2 convolution_subtract_fusion
  431.5 11.7 %cholesky.217 = f32[128,128]{1,0:T(8,128)S(1)} custom-call(f32[128,128]{1,0:T(8,128)S(1)} %cholesky.270), custom_call_target="Cholesky" | custom-call | tf_op jit(solution)/shard_map/jit(cholesky)/cholesky | solution.py:102
  443.9 9.9 custom-call.34
  454.8 1.4 convolution_subtract_fusion.1
  456.3 11.7 %cholesky.238 = f32[128,128]{1,0:T(8,128)S(1)} custom-call(f32[128,128]{1,0:T(8,128)S(1)} %cholesky.275), custom_call_target="Cholesky" | custom-call | tf_op jit(solution)/shard_map/jit(cholesky)/cholesky | solution.py:102
  469.3 9.8 custom-call.35
  480.0 1.4 convolution_subtract_fusion.2
  481.4 11.7 %cholesky.255 = f32[128,128]{1,0:T(8,128)S(1)} custom-call(f32[128,128]{1,0:T(8,128)S(1)} %convolution_subtract_fusion.2), custom_call_target="Cholesky" | custom-call | tf_op jit(solution)/shard_map/jit(cholesky)/cholesky | solution.py:102
  497.6 2.5 select_select_fusion
  500.2 11.2 %while.8 = (s32[]{:T(128)}, f32[512,512]{1,0:T(8,128)}, s32[4,2]{0,1:T(2,128)S(1)}, f32[4,128,128]{2,1,0:T(8,128)S(1)}, s32[]{:T(128)}) while((s32[]{:T(128)}, f32[512,512]{1,0:T(8,128)}, s32[4,2]{0,1:T(2,128)S(1)}, f32[4,128,128]{2,1,0:T(8,128)S(1)}, s32[]{:T(128)}) %tuple.52), condition=%wide.while_cond.1, body=%wide.while_body.1.sunk | while | flops 2 | bytes 131181 | solution.py:106
  500.8 2.2 bitcast_dynamic-update-slice_fusion.2
  503.6 2.2 bitcast_dynamic-update-slice_fusion.2
  506.4 2.2 bitcast_dynamic-update-slice_fusion.2
  509.3 2.1 bitcast_dynamic-update-slice_fusion.2
  511.4 39.3 %custom-call.39 = f32[4,128,128]{1,2,0:T(8,128)S(1)} custom-call(f32[4,128,128]{2,1,0:T(8,128)S(1)} %get-tuple-element.35), custom_call_target="InvertDiagBlocksLowerTriangular" | custom-call | tf_op jit(solution)/shard_map/triangular_solve/custom-call.8 | solution.py:106
  553.5 1.3 convolution_subtract_fusion.14
  557.7 1.2 convolution_subtract_fusion.11
  559.5 1.3 collective-permute-start.10
  560.8 2.9 collective-permute-done.10
  563.7 4.6 collective-permute-done.11
  568.3 4.0 collective-permute-done.12
  572.4 4.8 collective-permute-start.14
  577.2 2.3 collective-permute-done.13
  580.2 2.8 multiply_reduce_fusion.3
  584.4 83.4 %all-reduce.1 = (f32[2,32]{1,0:T(2,128)S(1)}, f32[2,32]{1,0:T(2,128)S(1)}) all-reduce(f32[2,32]{1,0:T(2,128)S(1)} %dynamic_update_slice.22, f32[2,32]{1,0:T(2,128)S(1)} %dynamic_update_slice.21), channel_id=1, replica_groups=mesh['blk'=32,'leaf'=4,'samp'=2] {'blk','leaf','samp'}, use_global_device_ids=true, to_apply=%region_13.18 | all-reduce | flops 128 | bytes 1024 | tf_op jit(solution)/shard_map/psum | solution.py:89
  667.9 160.6 %all-reduce.6.cloned.1.call-done = f32[2,512,32]{1,2,0:T(8,128)} async-done(((f32[2,512,32]{1,2,0:T(8,128)}), f32[2,512,32]{1,2,0:T(8,128)}) %all-reduce.6.cloned.1.call-update) | async-done | bytes 131088 | tf_op jit(solution)/shard_map/psum | solution.py:89
  832.2 1.3 convolution_subtract_fusion.8
  838.3 75.9 %psum.54 = f32[2,32]{1,0:T(2,128)S(1)} all-reduce(f32[2,32]{1,0:T(2,128)S(1)} %dynamic_update_slice.24), channel_id=1, replica_groups=mesh['blk'=32,'leaf'=4,'samp'=2] {'blk','leaf','samp'}, use_global_device_ids=true, to_apply=%region_16.21 | all-reduce | flops 64 | bytes 512 | tf_op jit(solution)/shard_map/psum | solution.py:89
  914.4 4.0 collective-permute-done.15
  918.3 4.0 collective-permute-done.16
  922.3 4.0 collective-permute-done.17
  927.1 4.1 collective-permute-start.19
  931.2 2.4 collective-permute-done.18
  934.2 2.0 multiply_reduce_fusion
  936.3 80.3 %psum.55 = f32[2,32]{1,0:T(2,128)S(1)} all-reduce(f32[2,32]{1,0:T(2,128)S(1)} %dynamic_update_slice.25), channel_id=1, replica_groups=mesh['blk'=32,'leaf'=4,'samp'=2] {'blk','leaf','samp'}, use_global_device_ids=true, to_apply=%region_18.23 | all-reduce | flops 64 | bytes 512 | tf_op jit(solution)/shard_map/psum | solution.py:89
  (152 shorter events, 36.2 us)
Async XLA Ops:
  7.2 393.1 %all-reduce.8.cloned.1.call-start = ((), (), s32[]{:S(2)}) async-start(), calls=%async_computation.1 | async-start | bytes 2359296 | tf_op jit(solution)/shard_map/psum | solution.py:100
  8.5 13.3 %collective-permute-start = (f32[512,256]{0,1:T(8,128)S(1)}, f32[512,256]{0,1:T(8,128)S(1)}, u32[]{:S(2)}, u32[]{:S(2)}) collective-permute-start(f32[512,256]{0,1:T(8,128)S(1)} %copy.10), channel_id=1, source_target_pairs={{0,2},{2,4},{4,6},{6,0},{1,3},{3,5},{5,7},{7,1},{8,10},{10,12},{12... | collective-permute-start | bytes 1572872 | tf_op jit(solution)/shard_map/ppermute | solution.py:18
  21.7 13.3 %collective-permute-start.1 = (f32[512,256]{0,1:T(8,128)S(1)}, f32[512,256]{0,1:T(8,128)S(1)}, u32[]{:S(2)}, u32[]{:S(2)}) collective-permute-start(f32[512,256]{0,1:T(8,128)S(1)} %collective-permute-done), channel_id=1, source_target_pairs={{0,2},{2,4},{4,6},{6,0},{1,3},{3,5},{5,7},{7,1},{8,10},{10,12},{12... | collective-permute-start | bytes 1572872 | tf_op jit(solution)/shard_map/ppermute | solution.py:18
  23.3 10.9 %collective-permute-start.5 = (f32[3,256]{1,0:T(4,128)}, f32[3,256]{1,0:T(4,128)S(1)}, u32[]{:S(2)}, u32[]{:S(2)}) collective-permute-start(f32[3,256]{1,0:T(4,128)} %param.13), channel_id=1, source_target_pairs={{0,2},{2,4},{4,6},{6,0},{1,3},{3,5},{5,7},{7,1},{8,10},{10,12},{12... | collective-permute-start | bytes 9224 | tf_op jit(solution)/shard_map/ppermute | solution.py:18
  34.2 3.7 collective-permute-start.6
  35.0 11.9 %collective-permute-start.2 = (f32[512,256]{0,1:T(8,128)S(1)}, f32[512,256]{0,1:T(8,128)S(1)}, u32[]{:S(2)}, u32[]{:S(2)}) collective-permute-start(f32[512,256]{0,1:T(8,128)S(1)} %collective-permute-done.1), channel_id=1, source_target_pairs={{0,2},{2,4},{4,6},{6,0},{1,3},{3,5},{5,7},{7,1},{8,10},{10,12},{12... | collective-permute-start | bytes 1572872 | tf_op jit(solution)/shard_map/ppermute | solution.py:18
  37.8 9.1 collective-permute-start.7
  47.3 11.5 %copy-start.10 = (f32[3,256]{1,0:T(4,128)S(1)}, f32[3,256]{1,0:T(4,128)}, u32[]{:S(2)}) copy-start(f32[3,256]{1,0:T(4,128)} %param.13) | copy-start | bytes 9220
  48.8 57.1 %collective-permute-start.3 = (f32[512,1024]{0,1:T(8,128)}, f32[512,1024]{0,1:T(8,128)}, u32[]{:S(2)}, u32[]{:S(2)}) collective-permute-start(f32[512,1024]{0,1:T(8,128)} %constant_dynamic-slice_fusion.6), channel_id=1, source_target_pairs={{248,0},{0,8},{8,16},{16,24},{24,32},{32,40},{40,48},{48,56},{56,6... | collective-permute-start | bytes 6291464 | tf_op jit(solution)/shard_map/ppermute | solution.py:27
  52.7 53.3 %collective-permute-start.4 = (f32[512,1024]{0,1:T(8,128)}, f32[512,1024]{0,1:T(8,128)}, u32[]{:S(2)}, u32[]{:S(2)}) collective-permute-start(f32[512,1024]{0,1:T(8,128)} %constant_dynamic-slice_fusion.6), channel_id=1, source_target_pairs={{8,0},{16,8},{24,16},{32,24},{40,32},{48,40},{56,48},{64,56},{72,6... | collective-permute-start | bytes 6291464 | tf_op jit(solution)/shard_map/ppermute | solution.py:27
  58.9 43.2 %collective-permute-start.8 = (f32[3,1024]{1,0:T(4,128)S(1)}, f32[3,1024]{1,0:T(4,128)S(1)}, u32[]{:S(2)}, u32[]{:S(2)}) collective-permute-start(f32[3,1024]{1,0:T(4,128)S(1)} %constant_dynamic-slice_fusion.5), channel_id=1, source_target_pairs={{248,0},{0,8},{8,16},{16,24},{24,32},{32,40},{40,48},{48,56},{56,6... | collective-permute-start | bytes 36872 | tf_op jit(solution)/shard_map/ppermute | solution.py:27
  59.0 43.1 %collective-permute-start.9 = (f32[3,1024]{1,0:T(4,128)S(1)}, f32[3,1024]{1,0:T(4,128)S(1)}, u32[]{:S(2)}, u32[]{:S(2)}) collective-permute-start(f32[3,1024]{1,0:T(4,128)S(1)} %constant_dynamic-slice_fusion.5), channel_id=1, source_target_pairs={{8,0},{16,8},{24,16},{32,24},{40,32},{48,40},{56,48},{64,56},{72,6... | collective-permute-start | bytes 36872 | tf_op jit(solution)/shard_map/ppermute | solution.py:27
  118.7 5.6 copy-start
  138.9 3.7 copy-start.4
  138.9 3.7 copy-start.11
  143.2 0.7 copy-start.6
  143.8 684.7 %all-reduce.6.cloned.1.call-start = ((), (), s32[]{:S(2)}) async-start(), calls=%async_computation | async-start | bytes 262144 | tf_op jit(solution)/shard_map/psum | solution.py:89
  404.6 1.0 copy-start.1
  456.2 94.5 %copy-start.8 = (f32[2,512,32]{1,2,0:T(8,128)S(1)}, f32[2,512,32]{1,2,0:T(8,128)}, u32[]{:S(2)}) copy-start(f32[2,512,32]{1,2,0:T(8,128)} %get-tuple-element.51) | copy-start | bytes 393220
  559.5 20.1 %copy-start.2 = (f32[32,256]{1,0:T(8,128)}, f32[32,256]{1,0:T(8,128)S(1)}, u32[]{:S(2)}) copy-start(f32[32,256]{1,0:T(8,128)S(1)} %convolution_subtract_fusion.4) | copy-start | bytes 98308
  559.5 4.2 collective-permute-start.10
  563.7 4.6 collective-permute-start.11
  568.3 4.0 collective-permute-start.12
  572.3 7.2 collective-permute-start.13
  572.4 7.1 collective-permute-start.14
  580.2 87.6 %copy-start.5 = (f32[32,256]{1,0:T(8,128)S(1)}, f32[32,256]{1,0:T(8,128)}, u32[]{:S(2)}) copy-start(f32[32,256]{1,0:T(8,128)} %param.17) | copy-start | bytes 98308
  580.2 248.3 %copy-start.9 = (f32[2,512,32]{1,2,0:T(8,128)S(1)}, f32[2,512,32]{1,2,0:T(8,128)}, u32[]{:S(2)}) copy-start(f32[2,512,32]{1,2,0:T(8,128)} %get-tuple-element.51) | copy-start | bytes 393220
  583.1 331.2 %copy-start.3 = (f32[32,256]{1,0:T(8,128)S(1)}, f32[32,256]{1,0:T(8,128)}, u32[]{:S(2)}) copy-start(f32[32,256]{1,0:T(8,128)} %copy-done.2) | copy-start | bytes 98308
  583.7 0.6 copy-start.7
  914.3 4.0 collective-permute-start.15
  918.3 4.0 collective-permute-start.16
  922.3 4.0 collective-permute-start.17
  926.4 7.2 collective-permute-start.18
  927.1 6.5 collective-permute-start.19
Sparse Core Ops, SparseCore 0:
  144.0 256.2 all-reduce.7
  584.5 244.0 all-reduce.5
